TPU v7x, 32 devices: a whole 2x2x4 slice. The times are simulated.
32 devices in a mesh: replica: 16 (over z, x, core), shard: 2 (over y).
Axes of the slice: x: 2, y: 2, z: 4, core: 2. Of those that a mesh axis runs over, the one named last changes fastest.
Arguments:
- tokens: bfloat16 [8192, 768], P(('replica', 'shard')), may hold values from -32 to 32
- lengths: int32 [32], P(('replica', 'shard')), may hold values from 1 to 256, 5120 in all
- cotangent: bfloat16 [8192, 768], P(('replica', 'shard')), may hold values from -6 to 6
- w_qkv: bfloat16 [768, 2304], P('shard'), may hold values from -0.14433757 to 0.14433757
- bias_q: bfloat16 [768], P('shard'), may hold values from -3 to 3
- bias_v: bfloat16 [768], P('shard'), may hold values from -3 to 3
- w_out: bfloat16 [768, 768], P('shard'), may hold values from -1.75 to 1.75
- bias_out: bfloat16 [768], P('shard'), may hold values from -3 to 3
- gain_attn: bfloat16 [768], P('shard'), may hold values from 0.5 to 1.5
- shift_attn: bfloat16 [768], P('shard'), may hold values from -3 to 3
- w_in: bfloat16 [768, 3072], P('shard'), may hold values from -0.21875 to 0.21875
- bias_in: bfloat16 [3072], P('shard'), may hold values from -3 to 3
- w_back: bfloat16 [3072, 768], P('shard'), may hold values from -0.109375 to 0.109375
- bias_back: bfloat16 [768], P('shard'), may hold values from -3 to 3
- gain_ffn: bfloat16 [768], P('shard'), may hold values from 0.5 to 1.5
- shift_ffn: bfloat16 [768], P('shard'), may hold values from -3 to 3
Outputs:
- block_out: bfloat16 [8192, 768], P(('replica', 'shard'))
- grad_tokens: float32 [8192, 768], P(('replica', 'shard'))
- grad_w_qkv: float32 [768, 2304], P('shard')
- grad_bias_q: float32 [768], P('shard')
- grad_bias_v: float32 [768], P('shard')
- grad_w_out: float32 [768, 768], P('shard')
- grad_bias_out: float32 [768], P('shard')
- grad_gain_attn: float32 [768], P('shard')
- grad_shift_attn: float32 [768], P('shard')
- grad_w_in: float32 [768, 3072], P('shard')
- grad_bias_in: float32 [3072], P('shard')
- grad_w_back: float32 [3072, 768], P('shard')
- grad_bias_back: float32 [768], P('shard')
- grad_gain_ffn: float32 [768], P('shard')
- grad_shift_ffn: float32 [768], P('shard')
Inputs may be any that keep to these rules, and one draw needn't show every extreme that they name: `lengths`: each sequence has at least one live token; the longest has exactly 256.
All inputs are finite; a program needn't handle non-finite values. No bound on the sum of `lengths` on one device may be relied on, other than what follows from the above.
Results may differ from a plain program's by a relative error of at most 0.012.
The roundings to bfloat16 on the way count: a program that leaves them out, or rounds other values in their place, can miss the bound.
Values may be sent and summed in bfloat16 or wider, within the bound.
A program may use at most 192 MiB of HBM per device.

v0:
```python
import jax
import jax.numpy as jnp
from jax import lax
from jax.sharding import PartitionSpec as P

HEADS = 12
HEAD_DIM = 64


def product(form, left, right):
    return jnp.einsum(form, left, right, preferred_element_type=jnp.float32)


def normalize(hidden):
    average = jnp.mean(hidden, axis=-1, keepdims=True)
    centred = hidden - average
    inv_std = lax.rsqrt(jnp.mean(centred * centred, axis=-1, keepdims=True) + 1e-12)
    return (centred * inv_std, inv_std)


def norm_back(grad_in, normed, inv_std, gain):
    grad_norm = grad_in * gain
    return inv_std * (
        grad_norm
        - jnp.mean(grad_norm, axis=-1, keepdims=True)
        - normed * jnp.mean(grad_norm * normed, axis=-1, keepdims=True)
    )


def gelu_slope(pre):
    return (
        0.5 * (1.0 + lax.erf(pre * 0.7071067811865476))
        + pre * jnp.exp(-0.5 * pre * pre) * 0.3989422804014327
    )


def on_device(
    tokens,
    lengths,
    cotangent,
    w_qkv,
    bias_q,
    bias_v,
    w_out,
    bias_out,
    gain_attn,
    shift_attn,
    w_in,
    bias_in,
    w_back,
    bias_back,
    gain_ffn,
    shift_ffn,
):
    bf16 = jnp.bfloat16
    f32 = jnp.float32
    full = (
        lax.all_gather(w_qkv, "shard", axis=0, tiled=True),
        lax.all_gather(bias_q, "shard", axis=0, tiled=True),
        lax.all_gather(bias_v, "shard", axis=0, tiled=True),
        lax.all_gather(w_out, "shard", axis=0, tiled=True),
        lax.all_gather(bias_out, "shard", axis=0, tiled=True),
        lax.all_gather(gain_attn, "shard", axis=0, tiled=True),
        lax.all_gather(shift_attn, "shard", axis=0, tiled=True),
        lax.all_gather(w_in, "shard", axis=0, tiled=True),
        lax.all_gather(bias_in, "shard", axis=0, tiled=True),
        lax.all_gather(w_back, "shard", axis=0, tiled=True),
        lax.all_gather(bias_back, "shard", axis=0, tiled=True),
        lax.all_gather(gain_ffn, "shard", axis=0, tiled=True),
        lax.all_gather(shift_ffn, "shard", axis=0, tiled=True),
    )
    f_qkv, f_bq, f_bv, f_out, f_bo, f_ga, f_sa, f_in, f_bi, f_back, f_bb, f_gf, f_sf = full
    group = lengths.shape[0]
    span = tokens.shape[0] // group
    width = tokens.shape[1]
    scale = HEAD_DIM ** (-0.5)
    factor = float(tokens.shape[0] * lax.axis_size("replica") * lax.axis_size("shard")) ** (-0.5)
    live = jnp.arange(span, dtype=jnp.int32)[None, :] < lengths[:, None]
    inputs = tokens.reshape(group, span, width)
    qkv = product("bld,de->ble", inputs, f_qkv)
    query = (qkv[..., :width] + f_bq.astype(f32)).astype(bf16).reshape(group, span, HEADS, HEAD_DIM)
    keys = qkv[..., width : 2 * width].astype(bf16).reshape(group, span, HEADS, HEAD_DIM)
    values = (
        (qkv[..., 2 * width :] + f_bv.astype(f32))
        .astype(bf16)
        .reshape(group, span, HEADS, HEAD_DIM)
    )

    def make_scores():
        raw = product("bqhe,bkhe->bhqk", query, keys) * scale
        return jnp.where(live[:, None, None, :], raw, -1000000000.0)

    scores = make_scores()
    top = jnp.max(scores, axis=-1, keepdims=True)
    expo = jnp.exp(scores - top)
    total = jnp.sum(expo, axis=-1, keepdims=True)
    log_total = top + jnp.log(total)
    attend = (expo / total).astype(bf16)
    context = product("bhqk,bkhe->bqhe", attend, values).reshape(group, span, width).astype(bf16)
    resid_one = inputs.astype(f32) + product("bld,de->ble", context, f_out) + f_bo.astype(f32)
    normed_one, inv_one = normalize(resid_one)
    gain_one = f_ga.astype(f32)
    mid = normed_one * gain_one + f_sa.astype(f32)
    mid_b = mid.astype(bf16)
    pre = product("bld,df->blf", mid_b, f_in) + f_bi.astype(f32)
    act = (0.5 * pre * (1.0 + lax.erf(pre * 0.7071067811865476))).astype(bf16)
    resid_two = mid + product("blf,fd->bld", act, f_back) + f_bb.astype(f32)
    normed_two, inv_two = normalize(resid_two)
    gain_two = f_gf.astype(f32)
    block_out = (normed_two * gain_two + f_sf.astype(f32)).astype(bf16)
    again = (
        lax.all_gather(w_qkv, "shard", axis=0, tiled=True),
        lax.all_gather(bias_q, "shard", axis=0, tiled=True),
        lax.all_gather(bias_v, "shard", axis=0, tiled=True),
        lax.all_gather(w_out, "shard", axis=0, tiled=True),
        lax.all_gather(bias_out, "shard", axis=0, tiled=True),
        lax.all_gather(gain_attn, "shard", axis=0, tiled=True),
        lax.all_gather(shift_attn, "shard", axis=0, tiled=True),
        lax.all_gather(w_in, "shard", axis=0, tiled=True),
        lax.all_gather(bias_in, "shard", axis=0, tiled=True),
        lax.all_gather(w_back, "shard", axis=0, tiled=True),
        lax.all_gather(bias_back, "shard", axis=0, tiled=True),
        lax.all_gather(gain_ffn, "shard", axis=0, tiled=True),
        lax.all_gather(shift_ffn, "shard", axis=0, tiled=True),
    )
    b_qkv = again[0]
    b_out = again[3]
    b_in = again[7]
    b_back = again[9]
    grad_out = cotangent.reshape(group, span, width).astype(f32) * live[..., None].astype(f32)
    g_gain_ffn = jnp.sum(grad_out * normed_two, axis=(0, 1))
    g_shift_ffn = jnp.sum(grad_out, axis=(0, 1))
    grad_two = norm_back(grad_out, normed_two, inv_two, gain_two)
    grad_two_b = grad_two.astype(bf16)
    g_w_back = product("blf,bld->fd", act, grad_two_b)
    g_bias_back = jnp.sum(grad_two, axis=(0, 1))
    grad_pre = product("bld,fd->blf", grad_two_b, b_back) * gelu_slope(pre)
    grad_pre_b = grad_pre.astype(bf16)
    g_w_in = product("bld,blf->df", mid_b, grad_pre_b)
    g_bias_in = jnp.sum(grad_pre, axis=(0, 1))
    grad_mid = grad_two + product("blf,df->bld", grad_pre_b, b_in)
    g_gain_attn = jnp.sum(grad_mid * normed_one, axis=(0, 1))
    g_shift_attn = jnp.sum(grad_mid, axis=(0, 1))
    grad_one = norm_back(grad_mid, normed_one, inv_one, gain_one)
    grad_one_b = grad_one.astype(bf16)
    g_w_out = product("bld,ble->de", context, grad_one_b)
    g_bias_out = jnp.sum(grad_one, axis=(0, 1))
    grad_ctx = (
        product("ble,de->bld", grad_one_b, b_out).astype(bf16).reshape(group, span, HEADS, HEAD_DIM)
    )
    weights_again = jnp.exp(make_scores() - log_total)
    weights_b = weights_again.astype(bf16)
    grad_att = product("bqhe,bkhe->bhqk", grad_ctx, values)
    grad_values = product("bhqk,bqhe->bkhe", weights_b, grad_ctx).reshape(group, span, width)
    delta = jnp.sum(weights_again * grad_att, axis=-1, keepdims=True)
    grad_scores = (weights_again * (grad_att - delta) * scale).astype(bf16)
    grad_query = product("bhqk,bkhe->bqhe", grad_scores, keys).reshape(group, span, width)
    grad_keys = product("bhqk,bqhe->bkhe", grad_scores, query).reshape(group, span, width)
    grad_qkv_b = jnp.concatenate([grad_query, grad_keys, grad_values], axis=-1).astype(bf16)
    g_w_qkv = product("bld,ble->de", inputs, grad_qkv_b)
    g_bias_q = jnp.sum(grad_query, axis=(0, 1))
    g_bias_v = jnp.sum(grad_values, axis=(0, 1))
    grad_input = grad_one + product("ble,de->bld", grad_qkv_b, b_qkv)
    shares = (
        lax.psum_scatter(g_w_qkv * factor, "shard", scatter_dimension=0, tiled=True),
        lax.psum_scatter(g_bias_q * factor, "shard", scatter_dimension=0, tiled=True),
        lax.psum_scatter(g_bias_v * factor, "shard", scatter_dimension=0, tiled=True),
        lax.psum_scatter(g_w_out * factor, "shard", scatter_dimension=0, tiled=True),
        lax.psum_scatter(g_bias_out * factor, "shard", scatter_dimension=0, tiled=True),
        lax.psum_scatter(g_gain_attn * factor, "shard", scatter_dimension=0, tiled=True),
        lax.psum_scatter(g_shift_attn * factor, "shard", scatter_dimension=0, tiled=True),
        lax.psum_scatter(g_w_in * factor, "shard", scatter_dimension=0, tiled=True),
        lax.psum_scatter(g_bias_in * factor, "shard", scatter_dimension=0, tiled=True),
        lax.psum_scatter(g_w_back * factor, "shard", scatter_dimension=0, tiled=True),
        lax.psum_scatter(g_bias_back * factor, "shard", scatter_dimension=0, tiled=True),
        lax.psum_scatter(g_gain_ffn * factor, "shard", scatter_dimension=0, tiled=True),
        lax.psum_scatter(g_shift_ffn * factor, "shard", scatter_dimension=0, tiled=True),
    )
    s_qkv, s_bq, s_bv, s_out, s_bo, s_ga, s_sa, s_in, s_bi, s_back, s_bb, s_gf, s_sf = shares
    summed = lax.psum(
        (s_qkv, s_bq, s_bv, s_out, s_bo, s_ga, s_sa, s_in, s_bi, s_back, s_bb, s_gf, s_sf),
        "replica",
    )
    r_qkv, r_bq, r_bv, r_out, r_bo, r_ga, r_sa, r_in, r_bi, r_back, r_bb, r_gf, r_sf = summed
    return (
        block_out.reshape(group * span, width),
        grad_input.reshape(group * span, width),
        r_qkv,
        r_bq,
        r_bv,
        r_out,
        r_bo,
        r_ga,
        r_sa,
        r_in,
        r_bi,
        r_back,
        r_bb,
        r_gf,
        r_sf,
    )


def solution(mesh):
    placed = (
        P(("replica", "shard"), None),
        P(("replica", "shard")),
        P(("replica", "shard"), None),
        P("shard", None),
        P("shard"),
        P("shard"),
        P("shard", None),
        P("shard"),
        P("shard"),
        P("shard"),
        P("shard", None),
        P("shard"),
        P("shard", None),
        P("shard"),
        P("shard"),
        P("shard"),
    )
    return jax.shard_map(
        on_device,
        mesh=mesh,
        in_specs=placed,
        out_specs=(
            P(("replica", "shard"), None),
            P(("replica", "shard"), None),
            P("shard", None),
            P("shard"),
            P("shard"),
            P("shard", None),
            P("shard"),
            P("shard"),
            P("shard"),
            P("shard", None),
            P("shard"),
            P("shard", None),
            P("shard"),
            P("shard"),
            P("shard"),
        ),
        check_vma=False,
    )
```

profile of v0, /device:TPU:0, one launch (start us, length us, event | category | flops | bytes accessed | tf_op | source)
XLA Modules:
  0.0 862.2 jit_solution(6676754043816239792)
XLA Ops:
  10.8 5.3 all-gather.1
  16.2 4.4 all-gather
  20.6 4.4 all-gather.2
  25.0 4.7 all-gather.3
  29.7 4.5 all-gather.4
  34.3 4.5 all-gather.6
  39.4 4.5 all-gather.7
  44.0 4.5 all-gather.8
  49.1 4.6 all-gather.5
  55.5 6.5 all-gather.14.cloned.1.call-done
  62.0 3.1 convolution_bitcast_fusion
  66.2 1.0 copy.55
  68.1 1.9 fusion.63
  71.1 1.4 fusion.34
  72.5 13.8 %all-gather.16.cloned.1.call-done = bf16[768,768]{1,0:T(8,128)(2,1)} async-done(((bf16[384,768]{1,0:T(8,128)(2,1)}), bf16[768,768]{1,0:T(8,128)(2,1)}) %all-gather.16.cloned.1.call-update) | async-done | bytes 1179664 | tf_op jit(solution)/shard_map/all_gather | solution.py:61
  86.3 2.0 fusion.64
  90.0 60.5 %all-gather.18.cloned.1.call-done = bf16[768,3072]{1,0:T(8,128)(2,1)} async-done(((bf16[384,3072]{1,0:T(8,128)(2,1)}), bf16[768,3072]{1,0:T(8,128)(2,1)}) %all-gather.18.cloned.1.call-update) | async-done | bytes 4718608 | tf_op jit(solution)/shard_map/all_gather | solution.py:65
  150.5 6.6 multiply_convert_fusion.1
  157.1 57.5 %all-gather.20.cloned.1.call-done = bf16[3072,768]{1,0:T(8,128)(2,1)} async-done(((bf16[1536,768]{1,0:T(8,128)(2,1)}), bf16[3072,768]{1,0:T(8,128)(2,1)}) %all-gather.20.cloned.1.call-update) | async-done | bytes 4718608 | tf_op jit(solution)/shard_map/all_gather | solution.py:67
  214.6 4.7 fusion.65
  219.5 1.0 multiply_reduce_fusion.1
  220.6 1.7 fusion.59
  222.3 3.0 fusion.68
  225.4 2.2 multiply_reduce_fusion.2
  229.4 1.9 convolution_multiply_fusion.3
  231.6 1.4 log_add_fusion
  232.9 2.8 convolution_convert_fusion
  235.7 1.9 copy.57
  237.6 3.5 fusion.69
  241.1 5.1 fusion.35
  246.2 5.7 fusion.62
  251.9 1.8 fusion.61
  254.4 4.0 multiply_bitcast_fusion
  258.5 1.0 copy-done.2
  260.1 5.2 convolution_multiply_fusion.1
  265.3 1.1 copy-done.7
  267.0 5.1 convolution_multiply_fusion
  272.2 81.9 %reduce-scatter.5.cloned.1.call-done = f32[384,2304]{0,1:T(8,128)} async-done(((f32[768,2304]{0,1:T(8,128)}), f32[384,2304]{0,1:T(8,128)}) %reduce-scatter.5.cloned.1.call-update) | async-done | bytes 3538960 | tf_op jit(solution)/shard_map/reduce_scatter | solution.py:165
  354.1 113.0 %reduce-scatter.9.cloned.1.call-done = f32[384,3072]{1,0:T(8,128)} async-done(((f32[768,3072]{1,0:T(8,128)}), f32[384,3072]{1,0:T(8,128)}) %reduce-scatter.9.cloned.1.call-update) | async-done | bytes 4718608 | tf_op jit(solution)/shard_map/reduce_scatter | solution.py:172
  467.1 113.0 %reduce-scatter.11.cloned.1.call-done = f32[1536,768]{1,0:T(8,128)} async-done(((f32[3072,768]{1,0:T(8,128)}), f32[1536,768]{1,0:T(8,128)}) %reduce-scatter.11.cloned.1.call-update) | async-done | bytes 4718608 | tf_op jit(solution)/shard_map/reduce_scatter | solution.py:174
  582.9 7.5 all-reduce.11
  591.0 62.7 %all-reduce.9 = (f32[384]{0:T(512)}, f32[384]{0:T(512)}, f32[384]{0:T(512)}, f32[384]{0:T(512)}, f32[384]{0:T(512)}, /*index=5*/f32[1536]{0:T(1024)}, f32[384]{0:T(512)}, f32[384]{0:T(512)}, f32[384]{0:T(512)}) all-reduce(f32[384]{0:T(512)S(1)} %dynamic-slice.1, ...), channel_id=1, replica_groups=mesh['replica'=16,'shard'=2] {'replica'}, use_global_device_ids=true, to_apply=%region_15.16 | all-reduce | flops 4608 | bytes 36864 | tf_op jit(solution)/shard_map/psum | solution.py:180
  653.8 4.1 convolution_add_fusion.2
  657.9 183.6 %all-reduce.14.cloned.1.call-done = (f32[384,2304]{0,1:T(8,128)}, f32[384,768]{1,0:T(8,128)}, f32[384,3072]{1,0:T(8,128)}, f32[1536,768]{1,0:T(8,128)}) async-done(((f32[384,2304]{0,1:T(8,128)}, f32[384,768]{1,0:T(8,128)}, f32[384,3072]{1,0:T(8,128)}, f32[1536,768]{1,0:T(8,128)}), (f32[384,2304]{0,1:T(8,128)}, f32[384,768]{1,0:T(8,128)}, f32[384,3072]{1,0:T(8,128)}, ...) | async-done | bytes 14155792 | tf_op jit(solution)/shard_map/psum | solution.py:180
  841.5 5.2 copy.61
  846.8 1.0 copy.71
  847.8 5.7 copy.72
  853.5 2.2 copy.73
  (191 shorter events, 17.1 us)
Async XLA Ops:
  7.2 3.6 copy-start.38
  7.2 8.9 %copy-start.39 = (bf16[384]{0:T(512)(128)(2,1)S(1)}, bf16[384]{0:T(512)(128)(2,1)}, u32[]{:S(2)}) copy-start(bf16[384]{0:T(512)(128)(2,1)} %param.21) | copy-start | bytes 2308
  7.2 13.3 %copy-start.40 = (bf16[384]{0:T(512)(128)(2,1)S(1)}, bf16[384]{0:T(512)(128)(2,1)}, u32[]{:S(2)}) copy-start(bf16[384]{0:T(512)(128)(2,1)} %param.23) | copy-start | bytes 2308
  7.2 17.8 %copy-start.41 = (bf16[384]{0:T(512)(128)(2,1)S(1)}, bf16[384]{0:T(512)(128)(2,1)}, u32[]{:S(2)}) copy-start(bf16[384]{0:T(512)(128)(2,1)} %param.24) | copy-start | bytes 2308
  7.2 22.5 %copy-start.42 = (bf16[384]{0:T(512)(128)(2,1)S(1)}, bf16[384]{0:T(512)(128)(2,1)}, u32[]{:S(2)}) copy-start(bf16[384]{0:T(512)(128)(2,1)} %param.25) | copy-start | bytes 2308
  7.2 54.8 %all-gather.14.cloned.1.call-start = ((), (), s32[]{:S(2)}) async-start(), calls=%async_computation.4 | async-start | bytes 5308416 | tf_op jit(solution)/shard_map/all_gather | solution.py:58
  8.0 26.3 %copy-start.43 = (bf16[384]{0:T(512)(128)(2,1)S(1)}, bf16[384]{0:T(512)(128)(2,1)}, u32[]{:S(2)}) copy-start(bf16[384]{0:T(512)(128)(2,1)} %param.29) | copy-start | bytes 2308
  8.0 31.4 %copy-start.44 = (bf16[384]{0:T(512)(128)(2,1)S(1)}, bf16[384]{0:T(512)(128)(2,1)}, u32[]{:S(2)}) copy-start(bf16[384]{0:T(512)(128)(2,1)} %param.30) | copy-start | bytes 2308
  8.0 36.0 %copy-start.45 = (bf16[384]{0:T(512)(128)(2,1)S(1)}, bf16[384]{0:T(512)(128)(2,1)}, u32[]{:S(2)}) copy-start(bf16[384]{0:T(512)(128)(2,1)} %param.31) | copy-start | bytes 2308
  8.0 41.1 %copy-start.34 = (bf16[1536]{0:T(1024)(128)(2,1)S(1)}, bf16[1536]{0:T(1024)(128)(2,1)}, u32[]{:S(2)}) copy-start(bf16[1536]{0:T(1024)(128)(2,1)} %param.27) | copy-start | bytes 9220
  8.0 54.0 %copy-start.5 = (bf16[256,768]{1,0:T(8,128)(2,1)S(1)}, bf16[256,768]{1,0:T(8,128)(2,1)}, u32[]{:S(2)}) copy-start(bf16[256,768]{1,0:T(8,128)(2,1)} %param.16) | copy-start | bytes 1179652
  8.0 78.3 %all-gather.16.cloned.1.call-start = ((), (), s32[]{:S(2)}) async-start(), calls=%async_computation.5 | async-start | bytes 1769472 | tf_op jit(solution)/shard_map/all_gather | solution.py:61
  8.8 141.8 %all-gather.18.cloned.1.call-start = ((), (), s32[]{:S(2)}) async-start(), calls=%async_computation.6 | async-start | bytes 7077888 | tf_op jit(solution)/shard_map/all_gather | solution.py:65
  9.5 205.1 %all-gather.20.cloned.1.call-start = ((), (), s32[]{:S(2)}) async-start(), calls=%async_computation.7 | async-start | bytes 7077888 | tf_op jit(solution)/shard_map/all_gather | solution.py:67
  10.1 262.1 %reduce-scatter.7.cloned.1.call-start = ((), (), s32[]{:S(2)}) async-start(), calls=%async_computation.9 | async-start | bytes 3538944 | tf_op jit(solution)/shard_map/reduce_scatter | solution.py:168
  68.1 3.0 copy-start.15
  88.3 139.3 %copy-start.23 = (f32[256]{0:T(256)}, f32[256]{0:T(256)S(1)}, u32[]{:S(2)}) copy-start(f32[256]{0:T(256)S(1)} %broadcast_multiply_fusion.14) | copy-start | bytes 3076
  214.6 7.7 slice-start.4
  214.6 4.9 copy-start.12
  214.6 4.9 copy-start.37
  214.6 6.0 copy-start.25
  214.6 7.7 slice-start.5
  219.3 3.0 copy-start.47
  220.6 4.8 slice-start.2
  222.3 3.1 copy-start.6
  222.3 3.0 copy-start.1
  222.3 3.0 copy-start.30
  222.3 3.0 slice-start.3
  225.4 4.0 copy-start.11
  231.3 122.8 %reduce-scatter.5.cloned.1.call-start = ((), (), s32[]{:S(2)}) async-start(), calls=%async_computation.8 | async-start | bytes 10616832 | tf_op jit(solution)/shard_map/reduce_scatter | solution.py:165
  258.4 208.6 %reduce-scatter.9.cloned.1.call-start = ((), (), s32[]{:S(2)}) async-start(), calls=%async_computation.10 | async-start | bytes 14155776 | tf_op jit(solution)/shard_map/reduce_scatter | solution.py:172
  265.3 314.8 %reduce-scatter.11.cloned.1.call-start = ((), (), s32[]{:S(2)}) async-start(), calls=%async_computation.11 | async-start | bytes 14155776 | tf_op jit(solution)/shard_map/reduce_scatter | solution.py:174
  272.1 569.4 %all-reduce.14.cloned.1.call-start = ((), (), s32[]{:S(2)}) async-start(), calls=%async_computation.12 | async-start | bytes 28311552 | tf_op jit(solution)/shard_map/psum | solution.py:180
  580.0 2.6 copy-start.33
  580.0 2.7 copy-start.36
  580.1 2.7 copy-start.26
  580.1 2.7 copy-start.27
  580.1 2.7 copy-start.35
  580.1 2.7 copy-start.28
  580.1 2.7 copy-start.29
  580.1 2.7 copy-start.32
  580.1 73.7 %copy-start.4 = (f32[256,768]{1,0:T(8,128)S(1)}, f32[256,768]{1,0:T(8,128)}, u32[]{:S(2)}) copy-start(f32[256,768]{1,0:T(8,128)} %copy-done.3) | copy-start | bytes 2359300
  580.1 73.7 %copy-start.10 = (bf16[1,256,12,64]{1,3,2,0:T(8,128)(2,1)S(1)}, bf16[1,256,12,64]{1,3,2,0:T(8,128)(2,1)}, u32[]{:S(2)}) copy-start(bf16[1,256,12,64]{1,3,2,0:T(8,128)(2,1)} %copy-done.9) | copy-start | bytes 1179652
  580.1 73.7 %copy-start.18 = (bf16[12,64,256]{2,1,0:T(8,128)(2,1)S(1)}, bf16[12,64,256]{2,1,0:T(8,128)(2,1)}, u32[]{:S(2)}) copy-start(bf16[12,64,256]{2,1,0:T(8,128)(2,1)} %fusion.35) | copy-start | bytes 1179652
  580.1 73.7 %copy-start.20 = (bf16[1,256,12,64]{1,3,2,0:T(8,128)(2,1)S(1)}, bf16[1,256,12,64]{1,3,2,0:T(8,128)(2,1)}, u32[]{:S(2)}) copy-start(bf16[1,256,12,64]{1,3,2,0:T(8,128)(2,1)} %get-tuple-element.100) | copy-start | bytes 1179652
  841.5 5.3 copy-start.16
  846.8 6.7 slice-start
  847.8 5.7 slice-start.1
  (15 other events, 20.7 us)
Sparse Core Ops, SparseCore 0:
  9.6 52.3 all-gather.13
  63.5 22.7 all-gather.15
  87.9 62.6 all-gather.17
  151.9 62.6 all-gather.19
  231.4 34.7 reduce-scatter.6
  268.4 85.6 reduce-scatter.4
  356.4 110.6 reduce-scatter.8
  469.4 110.6 reduce-scatter.10
  584.6 256.8 all-reduce.13
where the time goes:
time: 863 us; the launch traced here: 862 us
  waiting for transfers between devices  632 us (73%)
  blocking collectives  112 us (13%)
  matrix products  64 us (7%)
  local copies, waits for them, and re-layouts  28.7 us (3%)
  between operations  16.4 us (2%)
    psum x1, waiting for transfers between devices, on_device(): lax.psum((s_qkv, s_bq, s_bv, s_out, s_bo, s_ga, s_sa, s_in, s_bi, s_back,...  184 us
    reduce_scatter x1, waiting for transfers between devices, on_device(): lax.psum_scatter(g_w_back * factor, 'shard', scatter_dimension=0, tiled=T...  113 us
    reduce_scatter x1, waiting for transfers between devices, on_device(): lax.psum_scatter(g_w_in * factor, 'shard', scatter_dimension=0, tiled=True)  113 us
    reduce_scatter x1, waiting for transfers between devices, on_device(): lax.psum_scatter(g_w_qkv * factor, 'shard', scatter_dimension=0, tiled=True)  81.9 us
    dot_general x18, matrix products, product(): return jnp.einsum(form, left, right, preferred_element_type=jnp.float32)  64 us
    psum x1, blocking collectives, on_device(): lax.psum((s_qkv, s_bq, s_bv, s_out, s_bo, s_ga, s_sa, s_in, s_bi, s_back,...  62.7 us
    all_gather x1, waiting for transfers between devices, on_device(): lax.all_gather(w_in, 'shard', axis=0, tiled=True)  60.5 us
    all_gather x1, waiting for transfers between devices, on_device(): lax.all_gather(w_back, 'shard', axis=0, tiled=True)  57.5 us
  transfers between devices with their start and end apart: 9, of which 8 were waited for; matrix products, arithmetic and copies ran while one was open for 7% of the time, Pallas kernels for 0%

commit v1 on v0

--- a/solution.py
+++ b/solution.py
@@ -1,3 +1,4 @@
+import functools
 import jax
 import jax.numpy as jnp
 from jax import lax
@@ -5,6 +6,21 @@
 
 HEADS = 12
 HEAD_DIM = 64
+
+
+def lay_node(z, which_axis):
+    s_next, item_now = (lax.axis_size(which_axis), lax.axis_index(which_axis))
+    v_now, n_now = (z, 1)
+    while n_now < s_next:
+        h_now = lax.ppermute(v_now, which_axis, [(to_i, to_i ^ n_now) for to_i in range(s_next)])
+        small = jnp.concatenate([v_now, h_now], axis=0)
+        f_now = jnp.concatenate([h_now, v_now], axis=0)
+        v_now = jnp.where(item_now & n_now == 0, small, f_now)
+        n_now = 2 * n_now
+    return v_now
+
+
+keep_up_levels_all = functools.partial(lay_node, which_axis="shard")
 
 
 def product(form, left, right):
@@ -62,7 +78,7 @@
         lax.all_gather(bias_out, "shard", axis=0, tiled=True),
         lax.all_gather(gain_attn, "shard", axis=0, tiled=True),
         lax.all_gather(shift_attn, "shard", axis=0, tiled=True),
-        lax.all_gather(w_in, "shard", axis=0, tiled=True),
+        keep_up_levels_all(w_in),
         lax.all_gather(bias_in, "shard", axis=0, tiled=True),
         lax.all_gather(w_back, "shard", axis=0, tiled=True),
         lax.all_gather(bias_back, "shard", axis=0, tiled=True),

time: 863 us -> 893 us (1.035)
  blocking collectives: 112 us -> 193 us
  waiting for transfers between devices: 632 us -> 574 us
    all_gather x1, blocking collectives: 5.31 us -> 87.7 us  [on_device(): lax.all_gather(bias_q, 'shard', axis=0, tiled=True)]
    all_gather x1, waiting for transfers between devices: 57.5 us -> 28.8 us  [on_device(): lax.all_gather(w_back, 'shard', axis=0, tiled=True)]
    all_gather x1, waiting for transfers between devices: 13.8 us -> 0.01 us  [on_device(): lax.all_gather(w_out, 'shard', axis=0, tiled=True)]
    unnamed x131 -> x129, local copies, waits for them, and re-layouts: 22.5 us -> 23.1 us
  transfers between devices with their start and end apart: 9 -> 10, of which waited for: 8 -> 6; matrix products, arithmetic and copies ran while one was open for 7% -> 8% of each run, Pallas kernels for 0% -> 0%
where the time goes in v1:
time: 893 us
  waiting for transfers between devices  574 us (64%)
  blocking collectives  193 us (22%)
  matrix products  68.2 us (8%)
  local copies, waits for them, and re-layouts  29.3 us (3%)
  between operations  16.4 us (2%)
    psum x1, waiting for transfers between devices, on_device(): lax.psum((s_qkv, s_bq, s_bv, s_out, s_bo, s_ga, s_sa, s_in, s_bi, s_back,...  184 us
    reduce_scatter x1, waiting for transfers between devices, on_device(): lax.psum_scatter(g_w_in * factor, 'shard', scatter_dimension=0, tiled=True)  113 us
    reduce_scatter x1, waiting for transfers between devices, on_device(): lax.psum_scatter(g_w_back * factor, 'shard', scatter_dimension=0, tiled=T...  113 us
    all_gather x1, blocking collectives, on_device(): lax.all_gather(bias_q, 'shard', axis=0, tiled=True)  87.7 us
    reduce_scatter x1, waiting for transfers between devices, on_device(): lax.psum_scatter(g_w_qkv * factor, 'shard', scatter_dimension=0, tiled=True)  81.9 us
    dot_general x18, matrix products, product(): return jnp.einsum(form, left, right, preferred_element_type=jnp.float32)  68.2 us
    psum x1, blocking collectives, on_device(): lax.psum((s_qkv, s_bq, s_bv, s_out, s_bo, s_ga, s_sa, s_in, s_bi, s_back,...  62.8 us
    all_gather x1, waiting for transfers between devices, on_device(): lax.all_gather(w_in, 'shard', axis=0, tiled=True)  51.8 us
  transfers between devices with their start and end apart: 10, of which 6 were waited for; matrix products, arithmetic and copies ran while one was open for 8% of the time, Pallas kernels for 0%

profile of v1, /device:TPU:0, one launch (start us, length us, event | category | flops | bytes accessed | tf_op | source)
XLA Modules:
  0.0 892.7 jit_solution(7422767984354038672)
XLA Ops:
  9.5 3.1 collective-permute-start
  14.4 87.7 %all-gather.1 = bf16[2,1,384]{2,1,0:T(2,128)(2,1)S(1)} all-gather(bf16[1,1,384]{2,1,0:T(2,128)(2,1)S(1)} %reshape.402), channel_id=1, replica_groups=mesh['replica'=16,'shard'=2] {'shard'}, dimensions={0}, use_global_device_ids=true | all-gather | bytes 2304 | tf_op jit(solution)/shard_map/all_gather | solution.py:75
  102.2 4.4 all-gather
  106.6 4.4 all-gather.2
  111.0 4.5 all-gather.3
  115.6 4.5 all-gather.4
  120.2 4.4 all-gather.6
  125.1 4.3 all-gather.7
  129.5 4.4 all-gather.8
  134.5 4.4 all-gather.5
  139.6 3.1 convolution_bitcast_fusion
  142.9 0.9 copy.54
  143.8 1.0 copy.55
  145.7 1.9 fusion.76
  148.7 1.4 fusion.43
  150.1 2.0 fusion.77
  153.0 6.7 multiply_convert_fusion.1
  159.7 28.8 %all-gather.18.cloned.1.call-done = bf16[3072,768]{1,0:T(8,128)(2,1)} async-done(((bf16[1536,768]{1,0:T(8,128)(2,1)}), bf16[3072,768]{1,0:T(8,128)(2,1)}) %all-gather.18.cloned.1.call-update) | async-done | bytes 4718608 | tf_op jit(solution)/shard_map/all_gather | solution.py:83
  188.4 4.7 fusion.78
  193.4 1.0 multiply_reduce_fusion.1
  194.4 1.7 fusion.72
  197.0 3.7 fusion.81
  200.7 51.8 %all-gather.20.cloned.1.call-done = bf16[768,3072]{1,0:T(8,128)(2,1)} async-done(((bf16[384,3072]{1,0:T(8,128)(2,1)}), bf16[768,3072]{1,0:T(8,128)(2,1)}) %all-gather.20.cloned.1.call-update) | async-done | bytes 4718608 | tf_op jit(solution)/shard_map/all_gather | solution.py:135
  252.5 5.6 multiply_reduce_fusion.2
  259.9 1.9 convolution_multiply_fusion.2
  262.0 1.4 log_add_fusion
  263.4 2.8 convolution_convert_fusion
  266.2 1.9 copy.57
  268.1 3.5 fusion.82
  271.6 5.1 fusion.44
  276.7 5.7 fusion.75
  282.4 1.8 fusion.74
  284.9 4.0 multiply_bitcast_fusion
  288.9 1.0 copy-done.2
  290.5 5.2 convolution_multiply_fusion.1
  295.8 1.1 copy-done.7
  297.5 5.1 convolution_multiply_fusion
  302.7 81.9 %reduce-scatter.5.cloned.1.call-done = f32[384,2304]{0,1:T(8,128)} async-done(((f32[768,2304]{0,1:T(8,128)}), f32[384,2304]{0,1:T(8,128)}) %reduce-scatter.5.cloned.1.call-update) | async-done | bytes 3538960 | tf_op jit(solution)/shard_map/reduce_scatter | solution.py:181
  384.6 113.0 %reduce-scatter.9.cloned.1.call-done = f32[384,3072]{1,0:T(8,128)} async-done(((f32[768,3072]{1,0:T(8,128)}), f32[384,3072]{1,0:T(8,128)}) %reduce-scatter.9.cloned.1.call-update) | async-done | bytes 4718608 | tf_op jit(solution)/shard_map/reduce_scatter | solution.py:188
  497.6 113.0 %reduce-scatter.11.cloned.1.call-done = f32[1536,768]{1,0:T(8,128)} async-done(((f32[3072,768]{1,0:T(8,128)}), f32[1536,768]{1,0:T(8,128)}) %reduce-scatter.11.cloned.1.call-update) | async-done | bytes 4718608 | tf_op jit(solution)/shard_map/reduce_scatter | solution.py:190
  613.3 7.5 all-reduce.11
  621.5 62.8 %all-reduce.9 = (f32[384]{0:T(512)}, f32[384]{0:T(512)}, f32[384]{0:T(512)}, f32[384]{0:T(512)}, f32[384]{0:T(512)}, /*index=5*/f32[1536]{0:T(1024)}, f32[384]{0:T(512)}, f32[384]{0:T(512)}, f32[384]{0:T(512)}) all-reduce(f32[384]{0:T(512)S(1)} %dynamic-slice.1, ...), channel_id=1, replica_groups=mesh['replica'=16,'shard'=2] {'replica'}, use_global_device_ids=true, to_apply=%region_15.16 | all-reduce | flops 4608 | bytes 36864 | tf_op jit(solution)/shard_map/psum | solution.py:196
  684.3 4.1 convolution_add_fusion.1
  688.4 183.5 %all-reduce.14.cloned.1.call-done = (f32[384,2304]{0,1:T(8,128)}, f32[384,768]{1,0:T(8,128)}, f32[384,3072]{1,0:T(8,128)}, f32[1536,768]{1,0:T(8,128)}) async-done(((f32[384,2304]{0,1:T(8,128)}, f32[384,768]{1,0:T(8,128)}, f32[384,3072]{1,0:T(8,128)}, f32[1536,768]{1,0:T(8,128)}), (f32[384,2304]{0,1:T(8,128)}, f32[384,768]{1,0:T(8,128)}, f32[384,3072]{1,0:T(8,128)}, ...) | async-done | bytes 14155792 | tf_op jit(solution)/shard_map/psum | solution.py:196
  872.0 5.2 copy.61
  877.2 1.0 copy.71
  878.3 5.7 copy.72
  884.0 2.2 copy.73
  (190 shorter events, 15.7 us)
Async XLA Ops:
  7.2 7.2 copy-start.39
  7.2 95.0 %copy-start.40 = (bf16[384]{0:T(512)(128)(2,1)S(1)}, bf16[384]{0:T(512)(128)(2,1)}, u32[]{:S(2)}) copy-start(bf16[384]{0:T(512)(128)(2,1)} %param.21) | copy-start | bytes 2308
  7.2 99.4 %copy-start.41 = (bf16[384]{0:T(512)(128)(2,1)S(1)}, bf16[384]{0:T(512)(128)(2,1)}, u32[]{:S(2)}) copy-start(bf16[384]{0:T(512)(128)(2,1)} %param.23) | copy-start | bytes 2308
  7.2 103.8 %copy-start.42 = (bf16[384]{0:T(512)(128)(2,1)S(1)}, bf16[384]{0:T(512)(128)(2,1)}, u32[]{:S(2)}) copy-start(bf16[384]{0:T(512)(128)(2,1)} %param.24) | copy-start | bytes 2308
  7.2 108.3 %copy-start.43 = (bf16[384]{0:T(512)(128)(2,1)S(1)}, bf16[384]{0:T(512)(128)(2,1)}, u32[]{:S(2)}) copy-start(bf16[384]{0:T(512)(128)(2,1)} %param.25) | copy-start | bytes 2308
  7.2 132.3 %all-gather.14.cloned.1.call-start = ((), (), s32[]{:S(2)}) async-start(), calls=%async_computation.4 | async-start | bytes 5308416 | tf_op jit(solution)/shard_map/all_gather | solution.py:74
  8.0 112.2 %copy-start.44 = (bf16[384]{0:T(512)(128)(2,1)S(1)}, bf16[384]{0:T(512)(128)(2,1)}, u32[]{:S(2)}) copy-start(bf16[384]{0:T(512)(128)(2,1)} %param.29) | copy-start | bytes 2308
  8.0 117.2 %copy-start.45 = (bf16[384]{0:T(512)(128)(2,1)S(1)}, bf16[384]{0:T(512)(128)(2,1)}, u32[]{:S(2)}) copy-start(bf16[384]{0:T(512)(128)(2,1)} %param.30) | copy-start | bytes 2308
  8.0 121.5 %copy-start.46 = (bf16[384]{0:T(512)(128)(2,1)S(1)}, bf16[384]{0:T(512)(128)(2,1)}, u32[]{:S(2)}) copy-start(bf16[384]{0:T(512)(128)(2,1)} %param.31) | copy-start | bytes 2308
  8.0 126.5 %copy-start.35 = (bf16[1536]{0:T(1024)(128)(2,1)S(1)}, bf16[1536]{0:T(1024)(128)(2,1)}, u32[]{:S(2)}) copy-start(bf16[1536]{0:T(1024)(128)(2,1)} %param.27) | copy-start | bytes 9220
  8.0 131.6 %copy-start.5 = (bf16[256,768]{1,0:T(8,128)(2,1)S(1)}, bf16[256,768]{1,0:T(8,128)(2,1)}, u32[]{:S(2)}) copy-start(bf16[256,768]{1,0:T(8,128)(2,1)} %param.16) | copy-start | bytes 1179652
  8.0 142.1 %all-gather.16.cloned.1.call-start = ((), (), s32[]{:S(2)}) async-start(), calls=%async_computation.5 | async-start | bytes 1769472 | tf_op jit(solution)/shard_map/all_gather | solution.py:77
  8.8 179.7 %all-gather.18.cloned.1.call-start = ((), (), s32[]{:S(2)}) async-start(), calls=%async_computation.6 | async-start | bytes 7077888 | tf_op jit(solution)/shard_map/all_gather | solution.py:83
  9.5 243.0 %all-gather.20.cloned.1.call-start = ((), (), s32[]{:S(2)}) async-start(), calls=%async_computation.7 | async-start | bytes 7077888 | tf_op jit(solution)/shard_map/all_gather | solution.py:135
  9.5 142.8 %collective-permute-start = (bf16[384,3072]{1,0:T(8,128)(2,1)}, bf16[384,3072]{1,0:T(8,128)(2,1)}, u32[]{:S(2)}, u32[]{:S(2)}) collective-permute-start(bf16[384,3072]{1,0:T(8,128)(2,1)} %param.26), channel_id=1, source_target_pairs={{0,1},{1,0},{2,3},{3,2},{4,5},{5,4},{6,7},{7,6},{8,9},{9,8},{10,11... | collective-permute-start | bytes 7077896 | tf_op jit(solution)/shard_map/ppermute | solution.py:15
  12.6 290.0 %reduce-scatter.7.cloned.1.call-start = ((), (), s32[]{:S(2)}) async-start(), calls=%async_computation.9 | async-start | bytes 3538944 | tf_op jit(solution)/shard_map/reduce_scatter | solution.py:184
  145.7 3.0 copy-start.14
  150.1 2.9 copy-start.33
  152.1 106.0 %copy-start.22 = (f32[256]{0:T(256)}, f32[256]{0:T(256)S(1)}, u32[]{:S(2)}) copy-start(f32[256]{0:T(256)S(1)} %broadcast_multiply_fusion.14) | copy-start | bytes 3076
  188.4 8.6 slice-start.2
  188.4 4.9 copy-start.12
  188.4 4.9 copy-start.38
  188.4 5.9 copy-start.24
  188.4 8.6 slice-start.3
  193.1 3.9 copy-start.48
  197.0 55.5 %copy-start.30 = (f32[256]{0:T(256)S(1)}, f32[256]{0:T(256)}, u32[]{:S(2)}) copy-start(f32[256]{0:T(256)} %copy-done.29) | copy-start | bytes 3076
  252.5 5.6 copy-start.1
  252.5 7.4 copy-start.11
  261.8 122.8 %reduce-scatter.5.cloned.1.call-start = ((), (), s32[]{:S(2)}) async-start(), calls=%async_computation.8 | async-start | bytes 10616832 | tf_op jit(solution)/shard_map/reduce_scatter | solution.py:181
  282.4 2.5 copy-start.18
  288.9 208.7 %reduce-scatter.9.cloned.1.call-start = ((), (), s32[]{:S(2)}) async-start(), calls=%async_computation.10 | async-start | bytes 14155776 | tf_op jit(solution)/shard_map/reduce_scatter | solution.py:188
  295.7 314.8 %reduce-scatter.11.cloned.1.call-start = ((), (), s32[]{:S(2)}) async-start(), calls=%async_computation.11 | async-start | bytes 14155776 | tf_op jit(solution)/shard_map/reduce_scatter | solution.py:190
  302.6 569.4 %all-reduce.14.cloned.1.call-start = ((), (), s32[]{:S(2)}) async-start(), calls=%async_computation.12 | async-start | bytes 28311552 | tf_op jit(solution)/shard_map/psum | solution.py:196
  610.5 2.6 copy-start.34
  610.5 2.7 copy-start.37
  610.5 2.7 copy-start.25
  610.5 2.7 copy-start.26
  610.5 2.7 copy-start.36
  610.6 2.7 copy-start.27
  610.6 2.7 copy-start.28
  610.6 2.7 copy-start.32
  610.6 73.7 %copy-start.4 = (f32[256,768]{1,0:T(8,128)S(1)}, f32[256,768]{1,0:T(8,128)}, u32[]{:S(2)}) copy-start(f32[256,768]{1,0:T(8,128)} %copy-done.3) | copy-start | bytes 2359300
  610.6 73.7 %copy-start.10 = (bf16[1,256,12,64]{1,3,2,0:T(8,128)(2,1)S(1)}, bf16[1,256,12,64]{1,3,2,0:T(8,128)(2,1)}, u32[]{:S(2)}) copy-start(bf16[1,256,12,64]{1,3,2,0:T(8,128)(2,1)} %copy-done.9) | copy-start | bytes 1179652
  610.6 73.7 %copy-start.17 = (bf16[12,64,256]{2,1,0:T(8,128)(2,1)S(1)}, bf16[12,64,256]{2,1,0:T(8,128)(2,1)}, u32[]{:S(2)}) copy-start(bf16[12,64,256]{2,1,0:T(8,128)(2,1)} %fusion.44) | copy-start | bytes 1179652
  610.6 73.7 %copy-start.19 = (bf16[1,256,12,64]{1,3,2,0:T(8,128)(2,1)S(1)}, bf16[1,256,12,64]{1,3,2,0:T(8,128)(2,1)}, u32[]{:S(2)}) copy-start(bf16[1,256,12,64]{1,3,2,0:T(8,128)(2,1)} %get-tuple-element.100) | copy-start | bytes 1179652
  872.0 5.3 copy-start.15
  877.2 6.7 slice-start
  878.3 5.7 slice-start.1
  (15 other events, 17.4 us)
Sparse Core Ops, SparseCore 0:
  9.6 90.0 all-gather.13
  101.2 22.8 all-gather.15
  125.7 62.6 all-gather.17
  189.8 62.6 all-gather.19
  261.9 34.7 reduce-scatter.6
  298.9 85.6 reduce-scatter.4
  386.9 110.6 reduce-scatter.8
  499.9 110.6 reduce-scatter.10
  615.1 256.8 all-reduce.13
